TPU v7x, 32 devices: a whole 2x2x4 slice. The times are simulated.
32 devices in a mesh: grp: 8 (over z, x), seq: 4 (over y, core).
Axes of the slice: x: 2, y: 2, z: 4, core: 2. Of those that a mesh axis runs over, the one named last changes fastest.
Arguments:
- frames_in: bfloat16 [8192, 512], P(('grp', 'seq')), may hold values from -6 to 6
- norm_gain: float32 [512], replicated, may hold values from 0.25 to 1.75
- qkv_weight: bfloat16 [512, 1536], replicated, may hold values from -0.25 to 0.25
- conv_weight: float32 [4, 1536], replicated, may hold values from -3 to 3
- out_weight: bfloat16 [512, 512], replicated, may hold values from -0.25 to 0.25
- head_gain: float32 [512], replicated, may hold values from 0.25 to 1.75
- ffn_gain: float32 [512], replicated, may hold values from 0.25 to 1.75
- up_weight: bfloat16 [512, 2048], P(None, 'seq'), may hold values from -0.25 to 0.25
- down_weight: bfloat16 [2048, 512], P('seq'), may hold values from -0.125 to 0.125
Outputs:
- encoded: bfloat16 [8192, 512], P(('grp', 'seq'))
All inputs are finite; a program needn't handle non-finite values.
Results may differ from a plain program's by a relative error of at most 0.007.
Values may be sent and summed in bfloat16 or wider, within the bound.
No kernel may reach another device: no remote copies, remote signals or barrier semaphores. Data moves between devices by JAX's collectives and lax.ppermute only.
A program may use at most 256 MiB of HBM per device.

v0:
```python
import jax
import jax.numpy as jnp
from jax import lax
from jax.sharding import PartitionSpec as P

HEADS = 8
HEAD = 64
KERNEL = 4
BLOCK = 256
EPSILON = 1e-05


def from_behind(block, axis, distance):
    devices = range(lax.axis_size(axis))
    route = [(i - distance, i) for i in devices if i - distance in devices]
    return lax.ppermute(block, axis, route)


def prefix_2(x, axis, combine, identity):
    length, place = (lax.axis_size(axis), lax.axis_index(axis))
    everything = lax.all_gather(x, axis)
    start = jnp.broadcast_to(jnp.asarray(identity, x.dtype), x.shape)

    def turn(k, before):
        reached = k < place
        new = combine(before, everything[k])
        return jnp.where(reached, new, before)

    return lax.fori_loop(0, length, turn, start)


def rms_scale(values_in, gain):
    mean_square = jnp.mean(values_in * values_in, axis=-1, keepdims=True)
    return values_in * lax.rsqrt(mean_square + EPSILON) * gain


def add_states(earlier, later):
    return earlier + later


def attend_block(pieces):
    queries, key_rows, value_rows, state_low = pieces
    block_len = queries.shape[0]
    causal = jnp.arange(block_len)[:, None] >= jnp.arange(block_len)[None, :]
    scores = jnp.einsum("thd,shd->hts", queries, key_rows, preferred_element_type=jnp.float32)
    scores = jnp.where(causal[None], scores, 0.0).astype(jnp.bfloat16)
    local_part = jnp.einsum("hts,shd->thd", scores, value_rows, preferred_element_type=jnp.float32)
    carried_part = jnp.einsum(
        "thd,hde->the", queries, state_low, preferred_element_type=jnp.float32
    )
    return local_part + carried_part


def body(
    frames_in,
    norm_gain,
    qkv_weight,
    conv_weight,
    out_weight,
    head_gain,
    ffn_gain,
    up_weight,
    down_weight,
):
    row_count, model_width = frames_in.shape
    block_count = row_count // BLOCK
    lag_rows = KERNEL - 1
    normed = rms_scale(frames_in.astype(jnp.float32), norm_gain).astype(jnp.bfloat16)
    projected = jnp.dot(normed, qkv_weight, preferred_element_type=jnp.float32).astype(jnp.bfloat16)
    before = from_behind(projected[row_count - lag_rows :], ("grp", "seq"), 1)
    extended = jnp.concatenate([before, projected], axis=0).astype(jnp.float32)
    convolved = jnp.zeros((row_count, 3 * model_width), jnp.float32)
    for offset in range(KERNEL):
        convolved = (
            convolved
            + conv_weight[offset] * extended[lag_rows - offset : lag_rows - offset + row_count]
        )
    block_shape = (block_count, BLOCK, HEADS, HEAD)
    queries = jax.nn.silu(convolved[:, :model_width]).astype(jnp.bfloat16).reshape(block_shape)
    key_rows = (
        jax.nn.silu(convolved[:, model_width : 2 * model_width])
        .astype(jnp.bfloat16)
        .reshape(block_shape)
    )
    value_rows = convolved[:, 2 * model_width :].astype(jnp.bfloat16).reshape(block_shape)
    block_states = jnp.einsum(
        "bshd,bshe->bhde", key_rows, value_rows, preferred_element_type=jnp.float32
    )
    device_state = jnp.sum(block_states, axis=0)
    zero_state = jnp.zeros_like(device_state)
    prefix = prefix_2(device_state, ("grp", "seq"), add_states, zero_state)
    earlier_blocks = jnp.concatenate(
        [zero_state[None], jnp.cumsum(block_states[:-1], axis=0)], axis=0
    )
    state_low = (prefix[None] + earlier_blocks).astype(jnp.bfloat16)
    attended = lax.map(attend_block, (queries, key_rows, value_rows, state_low))
    head_square = jnp.mean(attended * attended, axis=-1, keepdims=True)
    headed = (attended * lax.rsqrt(head_square + EPSILON)).reshape(
        row_count, model_width
    ) * head_gain
    headed = headed.astype(jnp.bfloat16)
    residual = frames_in.astype(jnp.float32) + jnp.dot(
        headed, out_weight, preferred_element_type=jnp.float32
    )
    normed_ffn = rms_scale(residual, ffn_gain).astype(jnp.bfloat16)
    inner_act = jax.nn.gelu(
        jnp.dot(
            normed_ffn,
            lax.all_gather(up_weight, "seq", axis=1, tiled=True),
            preferred_element_type=jnp.float32,
        )
    ).astype(jnp.bfloat16)
    ffn_out = jnp.dot(
        inner_act,
        lax.all_gather(down_weight, "seq", axis=0, tiled=True),
        preferred_element_type=jnp.float32,
    )
    return (residual + ffn_out).astype(jnp.bfloat16)


def solution(mesh):
    in_specs = (
        P(("grp", "seq"), None),
        P(),
        P(),
        P(),
        P(),
        P(),
        P(),
        P(None, "seq"),
        P("seq", None),
    )
    out_specs = P(("grp", "seq"), None)
    return jax.shard_map(body, mesh=mesh, in_specs=in_specs, out_specs=out_specs, check_vma=False)
```

profile of v0, /device:TPU:0, one launch (start us, length us, event | category | flops | bytes accessed | tf_op | source)
XLA Modules:
  0.0 155.0 jit_solution(5738290194023966455)
XLA Ops:
  6.5 1.2 fusion.21
  8.0 1.6 %convolution_convert_fusion = bf16[256,1536]{1,0:T(8,128)(2,1)S(1)} fusion(bf16[512,1536]{1,0:T(8,128)(2,1)S(1)} %copy-done, bf16[256,512]{1,0:T(8,128)(2,1)} %param.11, f32[512]{0:T(512)} %param.12, f32[256]{0:T(256)S(1)} %add_rsqrt_fusion.2), kind=kOutput, calls=%fused_computation.2 | convolution fusion | flops 403570688 | bytes 2624512 | tf_op jit(solution)/shard_map/dot_general | solution.py:69
  9.6 2.4 %collective-permute-start = (bf16[3,1536]{1,0:T(4,128)(2,1)S(1)}, bf16[3,1536]{1,0:T(4,128)(2,1)S(1)}, u32[]{:S(2)}, u32[]{:S(2)}) collective-permute-start(bf16[3,1536]{1,0:T(4,128)(2,1)S(1)} %slice.49), channel_id=1, source_target_pairs={{0,1},{1,2},{2,3},{3,4},{4,5},{5,6},{6,7},{7,8},{8,9},{9,10},{10,1... | collective-permute-start | bytes 27656 | tf_op jit(solution)/shard_map/ppermute | solution.py:16
  12.1 0.7 collective-permute-done
  13.1 0.7 fusion.8
  13.7 0.3 multiply_convert_fusion.1
  14.3 0.9 fusion.40
  15.3 0.7 all-gather.5.cloned.1.call-update
  16.1 0.7 all-gather.7.cloned.1.call-update
  17.0 80.1 %all-gather.9.cloned.1.call-done = f32[256,64,64]{2,1,0:T(8,128)} async-done(((f32[8,64,64]{2,1,0:T(8,128)}), f32[256,64,64]{2,1,0:T(8,128)}) %all-gather.9.cloned.1.call-update) | async-done | bytes 4194320 | tf_op jit(solution)/shard_map/all_gather | solution.py:21
  97.0 34.4 %while.18 = (s32[]{:T(128)}, f32[8,64,64]{2,1,0:T(8,128)S(1)}, s32[]{:T(128)}, f32[32,8,64,64]{3,2,1,0:T(8,128)}, s32[]{:T(128)}, /*index=5*/s32[]{:T(128)}) while((s32[]{:T(128)}, f32[8,64,64]{2,1,0:T(8,128)S(1)}, s32[]{:T(128)}, f32[32,8,64,64]{3,2,1,0:T(8,128)}, s32[]{:T(128)}, /*index=5*/s32[]{:T(128)}) %tuple.49), condition=%wide.region_2.3_spmd.clone, body=%wide.region_1.2_spmd.clone.sunk | while | flops 98308 | bytes 393309 | solution.py:29
  97.0 1.0 add_select_fusion.2
  98.1 1.0 add_select_fusion.2
  99.2 1.0 add_select_fusion.2
  100.2 1.0 add_select_fusion.2
  101.3 1.0 add_select_fusion.2
  102.4 1.1 add_select_fusion.2
  103.5 1.1 add_select_fusion.2
  104.6 1.1 add_select_fusion.2
  105.7 1.0 add_select_fusion.2
  106.8 1.0 add_select_fusion.2
  107.9 1.0 add_select_fusion.2
  108.9 1.0 add_select_fusion.2
  110.0 1.0 add_select_fusion.2
  111.1 1.0 add_select_fusion.2
  112.1 1.0 add_select_fusion.2
  113.2 1.0 add_select_fusion.2
  114.3 1.0 add_select_fusion.2
  115.3 1.0 add_select_fusion.2
  116.4 1.0 add_select_fusion.2
  117.5 1.0 add_select_fusion.2
  118.6 1.0 add_select_fusion.2
  119.6 1.0 add_select_fusion.2
  120.7 1.0 add_select_fusion.2
  121.8 1.0 add_select_fusion.2
  122.8 1.0 add_select_fusion.2
  123.9 1.0 add_select_fusion.2
  125.0 1.0 add_select_fusion.2
  126.1 1.0 add_select_fusion.2
  127.1 1.1 add_select_fusion.2
  128.2 1.1 add_select_fusion.2
  129.3 1.1 add_select_fusion.2
  130.4 1.0 add_select_fusion.2
  131.5 1.1 fusion.33
  132.5 1.8 %multiply_reduce_fusion.1 = (f32[256,8]{0,1:T(8,128)S(1)}, f32[256,8,64]{0,2,1:T(8,128)S(1)}) fusion(f32[8,64,256]{2,1,0:T(8,128)} %fusion.33, bf16[256,8,64]{0,2,1:T(8,128)(2,1)S(1)} %bitcast.28, bf16[256,8,64]{0,2,1:T(8,128)(2,1)S(1)} %bitcast.30, bf16[256,8,64]{0,2,1:T(8,128)(2,1)S(1)} %bitcast.26, pred[256,256]{1,0:T(8,128)(4,1)S(1)} %iota_compare_fusion), kind=kOutput, calls=%fused_computation.41 | convolution fusion | flops 135657472 | bytes 1908736 | tf_op jit(solution)/shard_map/while/body/eval_jaxpr/hts,shd->thd/dot_general | solution.py:47
  134.6 1.5 multiply_reduce_fusion
  136.1 7.9 %all-gather.7.cloned.1.call-done = bf16[2048,512]{1,0:T(8,128)(2,1)} async-done(((bf16[512,512]{1,0:T(8,128)(2,1)}), bf16[2048,512]{1,0:T(8,128)(2,1)}) %all-gather.7.cloned.1.call-update) | async-done | bytes 2097168 | tf_op jit(solution)/shard_map/all_gather | solution.py:115
  144.0 4.5 %fusion.14 = bf16[256,512]{1,0:T(8,128)(2,1)} fusion(f32[256,512]{1,0:T(8,128)S(1)} %get-tuple-element.135, bf16[2048,512]{1,0:T(8,128)(2,1)} %all-gather.7.cloned.1.call-done, bf16[512,2048]{1,0:T(8,128)(2,1)} %all-gather.5.cloned.1.call-done, f32[512]{0:T(512)S(1)} %copy-done.4, f32[256]{0:T(256)S(1)} %add_rsqrt_fusion.1), kind=kOutput, calls=%fused_computation.24 | convolution fusion | flops 1079115776 | bytes 4983808 | tf_op jit(solution)/shard_map/dot_general | solution.py:113
  (29 shorter events, 1.4 us)
Async XLA Ops:
  6.5 1.5 copy-start
  6.5 5.5 %copy-start.2 = (f32[4,1536]{1,0:T(4,128)S(1)}, f32[4,1536]{1,0:T(4,128)}, u32[]{:S(2)}) copy-start(f32[4,1536]{1,0:T(4,128)} %param.14) | copy-start | bytes 73732
  6.5 90.5 %all-gather.9.cloned.1.call-start = ((), (), s32[]{:S(2)}) async-start(), calls=%async_computation.2 | async-start | bytes 8650752 | tf_op jit(solution)/shard_map/all_gather | solution.py:21
  9.6 3.2 %collective-permute-start = (bf16[3,1536]{1,0:T(4,128)(2,1)S(1)}, bf16[3,1536]{1,0:T(4,128)(2,1)S(1)}, u32[]{:S(2)}, u32[]{:S(2)}) collective-permute-start(bf16[3,1536]{1,0:T(4,128)(2,1)S(1)} %slice.49), channel_id=1, source_target_pairs={{0,1},{1,2},{2,3},{3,4},{4,5},{5,6},{6,7},{7,8},{8,9},{9,10},{10,1... | collective-permute-start | bytes 27656 | tf_op jit(solution)/shard_map/ppermute | solution.py:16
  15.3 120.8 %all-gather.5.cloned.1.call-start = ((), (), s32[]{:S(2)}) async-start(), calls=%async_computation | async-start | bytes 2621440 | tf_op jit(solution)/shard_map/all_gather | solution.py:109
  16.0 127.9 %all-gather.7.cloned.1.call-start = ((), (), s32[]{:S(2)}) async-start(), calls=%async_computation.1 | async-start | bytes 2621440 | tf_op jit(solution)/shard_map/all_gather | solution.py:115
  131.4 3.0 %copy-start.3 = (f32[512]{0:T(512)S(1)}, f32[512]{0:T(512)}, u32[]{:S(2)}) copy-start(f32[512]{0:T(512)} %param.16) | copy-start | bytes 6148
  132.5 2.1 %copy-start.1 = (bf16[256,512]{1,0:T(8,128)(2,1)S(1)}, bf16[256,512]{1,0:T(8,128)(2,1)}, u32[]{:S(2)}) copy-start(bf16[256,512]{1,0:T(8,128)(2,1)} %param.11) | copy-start | bytes 786436
  134.4 9.6 %copy-start.4 = (f32[512]{0:T(512)S(1)}, f32[512]{0:T(512)}, u32[]{:S(2)}) copy-start(f32[512]{0:T(512)} %param.17) | copy-start | bytes 6148
Sparse Core Ops, SparseCore 0:
  15.4 81.5 all-gather.8
  98.6 21.1 all-gather.4
  121.4 22.5 all-gather.6
where the time goes:
time: 156 us; the launch traced here: 155 us
  waiting for transfers between devices  90.1 us (58%)
  other arithmetic  36.2 us (23%)
  between operations  13.3 us (9%)
  matrix products  11.4 us (7%)
  starting transfers between devices  2.48 us (2%)
    all_gather x1, waiting for transfers between devices, prefix_2(): everything = lax.all_gather(x, axis)  80.1 us
    select_n x32, other arithmetic, turn(): return jnp.where(reached, new, before)  33.6 us
    all_gather x1, waiting for transfers between devices, body(): lax.all_gather(down_weight, 'seq', axis=0, tiled=True)  7.88 us
    dot_general x1, matrix products, body(): jnp.dot(inner_act, lax.all_gather(down_weight, 'seq', axis=0, tiled=True)...  4.54 us
  transfers between devices with their start and end apart: 4, of which 3 were waited for; matrix products, arithmetic and copies ran while one was open for 25% of the time, Pallas kernels for 0%

commit v1 on v0

--- a/solution.py
+++ b/solution.py
@@ -8,6 +8,18 @@
 KERNEL = 4
 BLOCK = 256
 EPSILON = 1e-05
+
+
+def gather_around(array, axis, dim):
+    ways, here, step = (lax.axis_size(axis), lax.axis_index(axis), array.shape[dim])
+    shape = [n * ways if d == dim else n for d, n in enumerate(array.shape)]
+    full = lax.dynamic_update_slice_in_dim(
+        jnp.zeros(shape, array.dtype), array, here * step, axis=dim
+    )
+    for far in range(1, ways):
+        array = lax.ppermute(array, axis, [(d, (d + 1) % ways) for d in range(ways)])
+        full = lax.dynamic_update_slice_in_dim(full, array, (here - far) % ways * step, axis=dim)
+    return full
 
 
 def from_behind(block, axis, distance):
@@ -111,9 +123,7 @@
         )
     ).astype(jnp.bfloat16)
     ffn_out = jnp.dot(
-        inner_act,
-        lax.all_gather(down_weight, "seq", axis=0, tiled=True),
-        preferred_element_type=jnp.float32,
+        inner_act, gather_around(down_weight, "seq", 0), preferred_element_type=jnp.float32
     )
     return (residual + ffn_out).astype(jnp.bfloat16)
 

time: 156 us -> 149 us (0.955)
  waiting for transfers between devices: 90.1 us -> 70.5 us
  local copies, waits for them, and re-layouts: 0.8 us -> 9.51 us
  starting transfers between devices: 2.48 us -> 5.62 us
    all_gather x1, waiting for transfers between devices: 80.1 us -> 49.1 us  [prefix_2(): everything = lax.all_gather(x, axis)]
    ppermute x0 -> x3, waiting for transfers between devices: none -> 20.6 us  [gather_around(): lax.ppermute(array, axis, [(d, (d + 1) % ways) for d in range(ways)])]
    all_gather x1 -> x0, waiting for transfers between devices: 7.88 us -> none  [body(): lax.all_gather(down_weight, 'seq', axis=0, tiled=True)]
    dynamic_update_slice x0 -> x4, local copies, waits for them, and re-layouts: none -> 6.48 us  [the longest x3 5.63 us: gather_around(): lax.dynamic_update_slice_in_dim(full, array, (here - far) % ways * step,...]
    ppermute x0 -> x3, starting transfers between devices: none -> 3.18 us  [gather_around(): lax.ppermute(array, axis, [(d, (d + 1) % ways) for d in range(ways)])]
  transfers between devices with their start and end apart: 4 -> 6, of which waited for: 3 -> 5; matrix products, arithmetic and copies ran while one was open for 25% -> 31% of each run, Pallas kernels for 0% -> 0%
where the time goes in v1:
time: 149 us; the launch traced here: 148 us
  waiting for transfers between devices  70.5 us (47%)
  other arithmetic  36.2 us (24%)
  between operations  13.7 us (9%)
  matrix products  11.4 us (8%)
  local copies, waits for them, and re-layouts  9.51 us (6%)
  starting transfers between devices  5.62 us (4%)
    all_gather x1, waiting for transfers between devices, prefix_2(): everything = lax.all_gather(x, axis)  49.1 us
    select_n x32, other arithmetic, turn(): return jnp.where(reached, new, before)  33.6 us
    ppermute x3, waiting for transfers between devices, gather_around(): lax.ppermute(array, axis, [(d, (d + 1) % ways) for d in range(ways)])  20.6 us
    dynamic_update_slice x3, local copies, waits for them, and re-layouts, gather_around(): lax.dynamic_update_slice_in_dim(full, array, (here - far) % ways * step,...  5.63 us
    dot_general x1, matrix products, body(): jnp.dot(inner_act, gather_around(down_weight, 'seq', 0), preferred_elemen...  4.54 us
    ppermute x3, starting transfers between devices, gather_around(): lax.ppermute(array, axis, [(d, (d + 1) % ways) for d in range(ways)])  3.18 us
  transfers between devices with their start and end apart: 6, of which 5 were waited for; matrix products, arithmetic and copies ran while one was open for 31% of the time, Pallas kernels for 0%

profile of v1, /device:TPU:0, one launch (start us, length us, event | category | flops | bytes accessed | tf_op | source)
XLA Modules:
  0.0 147.7 jit_solution(13361155009467363885)
XLA Ops:
  6.5 1.2 fusion.21
  8.0 1.6 %convolution_convert_fusion = bf16[256,1536]{1,0:T(8,128)(2,1)S(1)} fusion(bf16[512,1536]{1,0:T(8,128)(2,1)S(1)} %copy-done, bf16[256,512]{1,0:T(8,128)(2,1)} %param.11, f32[512]{0:T(512)} %param.12, f32[256]{0:T(256)S(1)} %add_rsqrt_fusion.2), kind=kOutput, calls=%fused_computation.2 | convolution fusion | flops 403570688 | bytes 2624512 | tf_op jit(solution)/shard_map/dot_general | solution.py:81
  9.6 2.4 %collective-permute-start = (bf16[3,1536]{1,0:T(4,128)(2,1)S(1)}, bf16[3,1536]{1,0:T(4,128)(2,1)S(1)}, u32[]{:S(2)}, u32[]{:S(2)}) collective-permute-start(bf16[3,1536]{1,0:T(4,128)(2,1)S(1)} %slice.49), channel_id=1, source_target_pairs={{0,1},{1,2},{2,3},{3,4},{4,5},{5,6},{6,7},{7,8},{8,9},{9,10},{10,1... | collective-permute-start | bytes 27656 | tf_op jit(solution)/shard_map/ppermute | solution.py:28
  15.4 2.7 %collective-permute-start.1 = (bf16[512,512]{1,0:T(8,128)(2,1)S(1)}, bf16[512,512]{1,0:T(8,128)(2,1)S(1)}, u32[]{:S(2)}, u32[]{:S(2)}) collective-permute-start(bf16[512,512]{1,0:T(8,128)(2,1)S(1)} %copy-done.2), channel_id=1, source_target_pairs={{0,1},{1,2},{2,3},{3,0},{4,5},{5,6},{6,7},{7,4},{8,9},{9,10},{10,1... | collective-permute-start | bytes 1572872 | tf_op jit(solution)/shard_map/ppermute | solution.py:20
  18.0 7.9 %collective-permute-done.1 = bf16[512,512]{1,0:T(8,128)(2,1)S(1)} collective-permute-done((bf16[512,512]{1,0:T(8,128)(2,1)S(1)}, bf16[512,512]{1,0:T(8,128)(2,1)S(1)}, u32[]{:S(2)}, u32[]{:S(2)}) %collective-permute-start.1) | collective-permute-done | bytes 524320 | tf_op jit(solution)/shard_map/ppermute | solution.py:20
  27.2 10.1 %collective-permute-done.2 = bf16[512,512]{1,0:T(8,128)(2,1)} collective-permute-done((bf16[512,512]{1,0:T(8,128)(2,1)S(1)}, bf16[512,512]{1,0:T(8,128)(2,1)}, u32[]{:S(2)}, u32[]{:S(2)}) %collective-permute-start.2) | collective-permute-done | bytes 524320 | tf_op jit(solution)/shard_map/ppermute | solution.py:20
  37.4 1.4 broadcast_in_dim.42
  39.9 1.9 %constant_dynamic-update-slice_fusion.2 = bf16[2048,512]{1,0:T(8,128)(2,1)} fusion(bf16[2048,512]{1,0:T(8,128)(2,1)} %constant_dynamic-update-slice_fusion.3, bf16[512,512]{1,0:T(8,128)(2,1)} %copy-done.3, s32[]{:T(128)S(6)} %select_n.56), kind=kLoop, calls=%fused_computation.61 | loop fusion | bytes 1048580 | tf_op jit(solution)/shard_map/dynamic_update_slice | solution.py:21
  41.8 1.9 %constant_dynamic-update-slice_fusion.1 = bf16[2048,512]{1,0:T(8,128)(2,1)} fusion(bf16[2048,512]{1,0:T(8,128)(2,1)} %constant_dynamic-update-slice_fusion.2, bf16[512,512]{1,0:T(8,128)(2,1)} %collective-permute-done.2, s32[]{:T(128)S(6)} %select_n.58), kind=kLoop, calls=%fused_computation.60 | loop fusion | bytes 1048580 | tf_op jit(solution)/shard_map/dynamic_update_slice | solution.py:21
  43.6 2.6 %collective-permute-done.3 = bf16[512,512]{1,0:T(8,128)(2,1)} collective-permute-done((bf16[512,512]{1,0:T(8,128)(2,1)}, bf16[512,512]{1,0:T(8,128)(2,1)}, u32[]{:S(2)}, u32[]{:S(2)}) %collective-permute-start.3) | collective-permute-done | bytes 524320 | tf_op jit(solution)/shard_map/ppermute | solution.py:20
  46.2 1.9 %constant_dynamic-update-slice_fusion = bf16[2048,512]{1,0:T(8,128)(2,1)} fusion(bf16[2048,512]{1,0:T(8,128)(2,1)} %constant_dynamic-update-slice_fusion.1, bf16[512,512]{1,0:T(8,128)(2,1)} %collective-permute-done.3, s32[]{:T(128)S(6)} %select_n.60), kind=kLoop, calls=%fused_computation.59 | loop fusion | bytes 1048580 | tf_op jit(solution)/shard_map/dynamic_update_slice | solution.py:21
  48.1 49.1 %all-gather.6.cloned.1.call-done = f32[256,64,64]{2,1,0:T(8,128)} async-done(((f32[8,64,64]{2,1,0:T(8,128)}), f32[256,64,64]{2,1,0:T(8,128)}) %all-gather.6.cloned.1.call-update) | async-done | bytes 4194320 | tf_op jit(solution)/shard_map/all_gather | solution.py:33
  97.2 34.4 %while.18 = (s32[]{:T(128)}, f32[8,64,64]{2,1,0:T(8,128)S(1)}, s32[]{:T(128)}, f32[32,8,64,64]{3,2,1,0:T(8,128)}, s32[]{:T(128)}, /*index=5*/s32[]{:T(128)}) while((s32[]{:T(128)}, f32[8,64,64]{2,1,0:T(8,128)S(1)}, s32[]{:T(128)}, f32[32,8,64,64]{3,2,1,0:T(8,128)}, s32[]{:T(128)}, /*index=5*/s32[]{:T(128)}) %tuple.47), condition=%wide.region_2.3_spmd.clone, body=%wide.region_1.2_spmd.clone.sunk | while | flops 98308 | bytes 393317 | solution.py:41
  98.3 1.0 add_select_fusion.2
  99.4 1.0 add_select_fusion.2
  100.4 1.0 add_select_fusion.2
  101.5 1.0 add_select_fusion.2
  102.6 1.1 add_select_fusion.2
  103.7 1.1 add_select_fusion.2
  104.8 1.1 add_select_fusion.2
  105.9 1.0 add_select_fusion.2
  107.0 1.0 add_select_fusion.2
  108.1 1.0 add_select_fusion.2
  109.1 1.0 add_select_fusion.2
  110.2 1.0 add_select_fusion.2
  111.3 1.0 add_select_fusion.2
  112.3 1.0 add_select_fusion.2
  113.4 1.0 add_select_fusion.2
  114.5 1.0 add_select_fusion.2
  115.6 1.0 add_select_fusion.2
  116.6 1.0 add_select_fusion.2
  117.7 1.0 add_select_fusion.2
  118.8 1.0 add_select_fusion.2
  119.8 1.0 add_select_fusion.2
  120.9 1.0 add_select_fusion.2
  122.0 1.0 add_select_fusion.2
  123.1 1.0 add_select_fusion.2
  124.1 1.0 add_select_fusion.2
  125.2 1.0 add_select_fusion.2
  126.3 1.0 add_select_fusion.2
  127.3 1.0 add_select_fusion.2
  128.4 1.0 add_select_fusion.2
  129.5 1.0 add_select_fusion.2
  130.6 1.0 add_select_fusion.2
  131.6 1.1 fusion.33
  132.7 1.8 %multiply_reduce_fusion.1 = (f32[256,8]{0,1:T(8,128)S(1)}, f32[256,8,64]{0,2,1:T(8,128)S(1)}) fusion(f32[8,64,256]{2,1,0:T(8,128)} %fusion.33, bf16[256,8,64]{0,2,1:T(8,128)(2,1)S(1)} %bitcast.28, bf16[256,8,64]{0,2,1:T(8,128)(2,1)S(1)} %bitcast.30, bf16[256,8,64]{0,2,1:T(8,128)(2,1)S(1)} %bitcast.26, pred[256,256]{1,0:T(8,128)(4,1)S(1)} %iota_compare_fusion), kind=kOutput, calls=%fused_computation.41 | convolution fusion | flops 135657472 | bytes 1908736 | tf_op jit(solution)/shard_map/while/body/eval_jaxpr/hts,shd->thd/dot_general | solution.py:59
  134.8 1.4 multiply_reduce_fusion
  136.3 4.5 %fusion.14 = bf16[256,512]{1,0:T(8,128)(2,1)} fusion(f32[256,512]{1,0:T(8,128)S(1)} %get-tuple-element.135, bf16[2048,512]{1,0:T(8,128)(2,1)} %constant_dynamic-update-slice_fusion, bf16[512,2048]{1,0:T(8,128)(2,1)} %all-gather.4.cloned.1.call-done, f32[512]{0:T(512)S(1)} %copy-done.6, f32[256]{0:T(256)S(1)} %add_rsqrt_fusion.1), kind=kOutput, calls=%fused_computation.24 | convolution fusion | flops 1079115776 | bytes 4983808 | tf_op jit(solution)/shard_map/dot_general | solution.py:125
  (41 shorter events, 7.1 us)
Async XLA Ops:
  6.5 1.5 %copy-start = (bf16[512,1536]{1,0:T(8,128)(2,1)S(1)}, bf16[512,1536]{1,0:T(8,128)(2,1)}, u32[]{:S(2)}) copy-start(bf16[512,1536]{1,0:T(8,128)(2,1)} %param.13) | copy-start | bytes 4718596
  6.5 5.5 %copy-start.4 = (f32[4,1536]{1,0:T(4,128)S(1)}, f32[4,1536]{1,0:T(4,128)}, u32[]{:S(2)}) copy-start(f32[4,1536]{1,0:T(4,128)} %param.14) | copy-start | bytes 73732
  6.5 90.7 %all-gather.6.cloned.1.call-start = ((), (), s32[]{:S(2)}) async-start(), calls=%async_computation.1 | async-start | bytes 8650752 | tf_op jit(solution)/shard_map/all_gather | solution.py:33
  9.6 3.2 %collective-permute-start = (bf16[3,1536]{1,0:T(4,128)(2,1)S(1)}, bf16[3,1536]{1,0:T(4,128)(2,1)S(1)}, u32[]{:S(2)}, u32[]{:S(2)}) collective-permute-start(bf16[3,1536]{1,0:T(4,128)(2,1)S(1)} %slice.49), channel_id=1, source_target_pairs={{0,1},{1,2},{2,3},{3,4},{4,5},{5,6},{6,7},{7,8},{8,9},{9,10},{10,1... | collective-permute-start | bytes 27656 | tf_op jit(solution)/shard_map/ppermute | solution.py:28
  13.7 1.6 %copy-start.2 = (bf16[512,512]{1,0:T(8,128)(2,1)S(1)}, bf16[512,512]{1,0:T(8,128)(2,1)}, u32[]{:S(2)}) copy-start(bf16[512,512]{1,0:T(8,128)(2,1)} %param.19) | copy-start | bytes 1572868
  15.3 120.9 %all-gather.4.cloned.1.call-start = ((), (), s32[]{:S(2)}) async-start(), calls=%async_computation | async-start | bytes 2621440 | tf_op jit(solution)/shard_map/all_gather | solution.py:121
  15.4 10.6 %collective-permute-start.1 = (bf16[512,512]{1,0:T(8,128)(2,1)S(1)}, bf16[512,512]{1,0:T(8,128)(2,1)S(1)}, u32[]{:S(2)}, u32[]{:S(2)}) collective-permute-start(bf16[512,512]{1,0:T(8,128)(2,1)S(1)} %copy-done.2), channel_id=1, source_target_pairs={{0,1},{1,2},{2,3},{3,0},{4,5},{5,6},{6,7},{7,4},{8,9},{9,10},{10,1... | collective-permute-start | bytes 1572872 | tf_op jit(solution)/shard_map/ppermute | solution.py:20
  25.9 0.8 copy-start.3
  26.7 10.6 %collective-permute-start.2 = (bf16[512,512]{1,0:T(8,128)(2,1)S(1)}, bf16[512,512]{1,0:T(8,128)(2,1)}, u32[]{:S(2)}, u32[]{:S(2)}) collective-permute-start(bf16[512,512]{1,0:T(8,128)(2,1)S(1)} %collective-permute-done.1), channel_id=1, source_target_pairs={{0,1},{1,2},{2,3},{3,0},{4,5},{5,6},{6,7},{7,4},{8,9},{9,10},{10,1... | collective-permute-start | bytes 1572872 | tf_op jit(solution)/shard_map/ppermute | solution.py:20
  37.3 8.9 %collective-permute-start.3 = (bf16[512,512]{1,0:T(8,128)(2,1)}, bf16[512,512]{1,0:T(8,128)(2,1)}, u32[]{:S(2)}, u32[]{:S(2)}) collective-permute-start(bf16[512,512]{1,0:T(8,128)(2,1)} %collective-permute-done.2), channel_id=1, source_target_pairs={{0,1},{1,2},{2,3},{3,0},{4,5},{5,6},{6,7},{7,4},{8,9},{9,10},{10,1... | collective-permute-start | bytes 1572872 | tf_op jit(solution)/shard_map/ppermute | solution.py:20
  131.6 3.0 %copy-start.5 = (f32[512]{0:T(512)S(1)}, f32[512]{0:T(512)}, u32[]{:S(2)}) copy-start(f32[512]{0:T(512)} %param.16) | copy-start | bytes 6148
  132.7 2.1 %copy-start.1 = (bf16[256,512]{1,0:T(8,128)(2,1)S(1)}, bf16[256,512]{1,0:T(8,128)(2,1)}, u32[]{:S(2)}) copy-start(bf16[256,512]{1,0:T(8,128)(2,1)} %param.11) | copy-start | bytes 786436
  134.5 1.7 %copy-start.6 = (f32[512]{0:T(512)S(1)}, f32[512]{0:T(512)}, u32[]{:S(2)}) copy-start(f32[512]{0:T(512)} %param.17) | copy-start | bytes 6148
Sparse Core Ops, SparseCore 0:
  15.4 81.7 all-gather.5
  98.8 21.1 all-gather.3
